TPU v7x, 256 devices: a whole 4x4x8 slice. The times are simulated.
256 devices in a mesh: tm: 64 (over z_hi, y, x), head: 4 (over z_lo, core).
Axes of the slice: x: 4, y: 4, z: 8 (z_hi: 4, z_lo: 2; z = z_hi * 2 + z_lo), core: 2. Of those that a mesh axis runs over, the one named last changes fastest.
Arguments:
- query: bfloat16 [16384, 4096], P('tm', 'head'), may hold values from -200 to 200
- key_in: bfloat16 [16384, 4096], P('tm', 'head'), may hold values from -7 to 7
- value: bfloat16 [16384, 4096], P('tm', 'head'), may hold values from -6 to 6
- grad_out: bfloat16 [16384, 4096], P('tm', 'head'), may hold values from -6 to 6
- weights: bfloat16 [3, 4096, 4096], P(None, 'tm', 'head'), may hold values from -0.09375 to 0.09375
Outputs:
- grad_input_t: bfloat16 [4096, 16384], P('head', 'tm')
All inputs are finite; a program needn't handle non-finite values.
Results may differ from a plain program's by a relative error of at most 0.0091.
Values may be sent and summed in bfloat16 or wider, within the bound.
A program may use at most 256 MiB of HBM per device.

v0:
```python
import jax
import jax.numpy as jnp
from jax import lax
from jax.sharding import PartitionSpec as P

HD = 128


def temporal(q_heads, k_heads, v_heads, g_heads):
    scale = 1.0 / q_heads.shape[-1] ** 0.5
    scores = (
        jnp.einsum("fphd,gphd->phfg", q_heads, k_heads, preferred_element_type=jnp.float32) * scale
    )
    probs = jax.nn.softmax(scores, axis=-1)
    probs_b = probs.astype(jnp.bfloat16)
    attended = jnp.einsum("phfg,gphd->fphd", probs_b, v_heads, preferred_element_type=jnp.float32)
    delta = jnp.transpose(jnp.sum(g_heads.astype(jnp.float32) * attended, axis=-1), (1, 2, 0))
    grad_probs = jnp.einsum("fphd,gphd->phfg", g_heads, v_heads, preferred_element_type=jnp.float32)
    grad_scores = (probs * (grad_probs - delta[..., None])).astype(jnp.bfloat16)
    grad_value = jnp.einsum("phfg,fphd->gphd", probs_b, g_heads, preferred_element_type=jnp.float32)
    grad_query = (
        jnp.einsum("phfg,gphd->fphd", grad_scores, k_heads, preferred_element_type=jnp.float32)
        * scale
    )
    grad_key = (
        jnp.einsum("phfg,fphd->gphd", grad_scores, q_heads, preferred_element_type=jnp.float32)
        * scale
    )
    return (
        grad_query.astype(jnp.bfloat16),
        grad_key.astype(jnp.bfloat16),
        grad_value.astype(jnp.bfloat16),
    )


def per_device(query, key_in, value, grad_out, weights):
    tok_rows, width = query.shape
    head_count = width // HD

    def split_heads(array):
        return array.reshape(1, tok_rows, head_count, HD)

    sq = split_heads(query)
    sk = split_heads(key_in)
    sv = split_heads(value)
    sg = split_heads(grad_out)
    moved = (
        lax.all_to_all(sq, "tm", split_axis=1, concat_axis=0, tiled=True),
        lax.all_to_all(sk, "tm", split_axis=1, concat_axis=0, tiled=True),
        lax.all_to_all(sv, "tm", split_axis=1, concat_axis=0, tiled=True),
        lax.all_to_all(sg, "tm", split_axis=1, concat_axis=0, tiled=True),
    )
    grads = temporal(moved[0], moved[1], moved[2], moved[3])
    back = (
        lax.all_to_all(grads[0], "tm", split_axis=0, concat_axis=1, tiled=True),
        lax.all_to_all(grads[1], "tm", split_axis=0, concat_axis=1, tiled=True),
        lax.all_to_all(grads[2], "tm", split_axis=0, concat_axis=1, tiled=True),
    )
    stacked = jnp.stack(
        [
            back[0].reshape(tok_rows, width),
            back[1].reshape(tok_rows, width),
            back[2].reshape(tok_rows, width),
        ]
    )
    partial_sum = jnp.einsum(
        "mic,mtc->it",
        lax.all_gather(weights, "tm", axis=1, tiled=True),
        stacked,
        preferred_element_type=jnp.float32,
    )
    mine = lax.psum_scatter(partial_sum, "head", scatter_dimension=0, tiled=True)
    return mine.astype(jnp.bfloat16)


def solution(mesh):
    placed = (
        P("tm", "head"),
        P("tm", "head"),
        P("tm", "head"),
        P("tm", "head"),
        P(None, "tm", "head"),
    )
    return jax.shard_map(
        per_device, mesh=mesh, in_specs=placed, out_specs=P("head", "tm"), check_vma=False
    )
```

profile of v0, /device:TPU:1, one launch (start us, length us, event | category | flops | bytes accessed | tf_op | source)
XLA Modules:
  0.0 372.9 jit_solution(12953759409687776059)
XLA Ops:
  7.3 2.0 copy.45
  9.2 15.1 %all-to-all-start = ((bf16[1,256,8,128]{3,2,0,1:T(8,128)(2,1)}), bf16[1,256,8,128]{3,2,0,1:T(8,128)(2,1)S(1)}, u32[]{:S(2)}, u32[]{:S(2)}) async-start(bf16[1,256,8,128]{3,2,0,1:T(8,128)(2,1)} %bitcast.15), calls=%async_computation | async-start | bytes 1048576 | tf_op jit(solution)/shard_map/all_to_all | solution.py:48
  24.3 1.9 copy.46
  26.3 17.0 %all-to-all-done = bf16[1,256,8,128]{3,2,0,1:T(8,128)(2,1)S(1)} async-done(((bf16[1,256,8,128]{3,2,0,1:T(8,128)(2,1)}), bf16[1,256,8,128]{3,2,0,1:T(8,128)(2,1)S(1)}, u32[]{:S(2)}, u32[]{:S(2)}) %all-to-all-start) | async-done | bytes 524320 | tf_op jit(solution)/shard_map/all_to_all | solution.py:48
  43.3 9.4 %all-to-all-start.1 = ((bf16[1,256,8,128]{3,2,0,1:T(8,128)(2,1)}), bf16[1,256,8,128]{3,2,0,1:T(8,128)(2,1)S(1)}, u32[]{:S(2)}, u32[]{:S(2)}) async-start(bf16[1,256,8,128]{3,2,0,1:T(8,128)(2,1)} %bitcast.19), calls=%async_computation.1 | async-start | bytes 1048576 | tf_op jit(solution)/shard_map/all_to_all | solution.py:49
  53.6 13.5 %all-to-all-done.1 = bf16[1,256,8,128]{3,2,0,1:T(8,128)(2,1)S(1)} async-done(((bf16[1,256,8,128]{3,2,0,1:T(8,128)(2,1)}), bf16[1,256,8,128]{3,2,0,1:T(8,128)(2,1)S(1)}, u32[]{:S(2)}, u32[]{:S(2)}) %all-to-all-start.1) | async-done | bytes 524320 | tf_op jit(solution)/shard_map/all_to_all | solution.py:49
  67.0 4.9 %all-to-all-start.3 = ((bf16[1,256,8,128]{3,2,0,1:T(8,128)(2,1)}), bf16[1,256,8,128]{3,2,0,1:T(8,128)(2,1)S(1)}, u32[]{:S(2)}, u32[]{:S(2)}) async-start(bf16[1,256,8,128]{3,2,0,1:T(8,128)(2,1)} %bitcast.27), calls=%async_computation.3 | async-start | bytes 1048576 | tf_op jit(solution)/shard_map/all_to_all | solution.py:50
  72.8 30.1 %all-to-all-done.3 = bf16[1,256,8,128]{3,2,0,1:T(8,128)(2,1)S(1)} async-done(((bf16[1,256,8,128]{3,2,0,1:T(8,128)(2,1)}), bf16[1,256,8,128]{3,2,0,1:T(8,128)(2,1)S(1)}, u32[]{:S(2)}, u32[]{:S(2)}) %all-to-all-start.3) | async-done | bytes 524320 | tf_op jit(solution)/shard_map/all_to_all | solution.py:50
  103.0 6.8 %all-to-all-start.2 = ((bf16[1,256,8,128]{3,2,0,1:T(8,128)(2,1)}), bf16[1,256,8,128]{3,2,0,1:T(8,128)(2,1)S(1)}, u32[]{:S(2)}, u32[]{:S(2)}) async-start(bf16[1,256,8,128]{3,2,0,1:T(8,128)(2,1)} %bitcast.23), calls=%async_computation.2 | async-start | bytes 1048576 | tf_op jit(solution)/shard_map/all_to_all | solution.py:51
  110.4 13.6 %all-to-all-done.2 = bf16[1,256,8,128]{3,2,0,1:T(8,128)(2,1)S(1)} async-done(((bf16[1,256,8,128]{3,2,0,1:T(8,128)(2,1)}), bf16[1,256,8,128]{3,2,0,1:T(8,128)(2,1)S(1)}, u32[]{:S(2)}, u32[]{:S(2)}) %all-to-all-start.2) | async-done | bytes 524320 | tf_op jit(solution)/shard_map/all_to_all | solution.py:51
  124.6 2.1 fusion.10
  127.0 1.1 copy.38
  128.2 5.9 %all-to-all-start.5 = ((bf16[64,4,8,128]{3,2,1,0:T(8,128)(2,1)}), bf16[64,4,8,128]{3,2,1,0:T(8,128)(2,1)S(1)}, u32[]{:S(2)}, u32[]{:S(2)}) async-start(bf16[64,4,8,128]{3,2,1,0:T(8,128)(2,1)} %copy.38), calls=%async_computation.5 | async-start | bytes 1048576 | tf_op jit(solution)/shard_map/all_to_all | solution.py:56
  134.5 1.2 copy.36
  135.6 18.6 %all-to-all-done.5 = bf16[64,4,8,128]{3,2,1,0:T(8,128)(2,1)S(1)} async-done(((bf16[64,4,8,128]{3,2,1,0:T(8,128)(2,1)}), bf16[64,4,8,128]{3,2,1,0:T(8,128)(2,1)S(1)}, u32[]{:S(2)}, u32[]{:S(2)}) %all-to-all-start.5) | async-done | bytes 524320 | tf_op jit(solution)/shard_map/all_to_all | solution.py:56
  154.3 11.3 %all-to-all-start.4 = ((bf16[64,4,8,128]{3,2,1,0:T(8,128)(2,1)}), bf16[64,4,8,128]{3,2,1,0:T(8,128)(2,1)S(1)}, u32[]{:S(2)}, u32[]{:S(2)}) async-start(bf16[64,4,8,128]{3,2,1,0:T(8,128)(2,1)} %copy.36), calls=%async_computation.4 | async-start | bytes 1048576 | tf_op jit(solution)/shard_map/all_to_all | solution.py:55
  165.6 1.6 fusion.16
  168.3 17.4 %all-to-all-done.4 = bf16[64,4,8,128]{3,2,1,0:T(8,128)(2,1)S(1)} async-done(((bf16[64,4,8,128]{3,2,1,0:T(8,128)(2,1)}), bf16[64,4,8,128]{3,2,1,0:T(8,128)(2,1)S(1)}, u32[]{:S(2)}, u32[]{:S(2)}) %all-to-all-start.4) | async-done | bytes 524320 | tf_op jit(solution)/shard_map/all_to_all | solution.py:55
  185.7 6.5 %all-to-all-start.6 = ((bf16[64,4,8,128]{3,2,1,0:T(8,128)(2,1)}), bf16[64,4,8,128]{3,2,1,0:T(8,128)(2,1)S(1)}, u32[]{:S(2)}, u32[]{:S(2)}) async-start(bf16[64,4,8,128]{3,2,1,0:T(8,128)(2,1)} %copy.40), calls=%async_computation.6 | async-start | bytes 1048576 | tf_op jit(solution)/shard_map/all_to_all | solution.py:57
  193.0 19.5 %all-to-all-done.6 = bf16[64,4,8,128]{3,2,1,0:T(8,128)(2,1)S(1)} async-done(((bf16[64,4,8,128]{3,2,1,0:T(8,128)(2,1)}), bf16[64,4,8,128]{3,2,1,0:T(8,128)(2,1)S(1)}, u32[]{:S(2)}, u32[]{:S(2)}) %all-to-all-start.6) | async-done | bytes 524320 | tf_op jit(solution)/shard_map/all_to_all | solution.py:57
  212.7 24.6 %all-gather.2.cloned.1.call-done = bf16[3,4096,1024]{2,1,0:T(8,128)(2,1)} async-done(((bf16[3,64,1024]{2,1,0:T(8,128)(2,1)}), bf16[3,4096,1024]{2,1,0:T(8,128)(2,1)}) %all-gather.2.cloned.1.call-update) | async-done | bytes 25165840 | tf_op jit(solution)/shard_map/all_gather | solution.py:68
  237.3 13.8 %convolution_bitcast_fusion = f32[4096,256]{0,1:T(8,128)} fusion(bf16[3,4096,1024]{2,1,0:T(8,128)(2,1)} %all-gather.2.cloned.1.call-done, bf16[1,256,1024]{2,1,0:T(8,128)(2,1)S(1)} %stack_reshape.11, bf16[1,256,1024]{2,1,0:T(8,128)(2,1)S(1)} %stack_reshape.10, bf16[1,256,1024]{2,1,0:T(8,128)(2,1)S(1)} %stack_reshape.9), kind=kOutput, calls=%fused_computation.1 | convolution fusion | flops 6444023808 | bytes 30932992 | tf_op jit(solution)/shard_map/mic,mtc->it/dot_general | solution.py:66
  251.1 112.7 %reduce-scatter.2.cloned.1.call-done = f32[1024,256]{0,1:T(8,128)} async-done(((f32[4096,256]{0,1:T(8,128)}), f32[1024,256]{0,1:T(8,128)}) %reduce-scatter.2.cloned.1.call-update) | async-done | bytes 1048592 | tf_op jit(solution)/shard_map/reduce_scatter | solution.py:72
  363.8 1.3 convert_element_type.39
  (21 shorter events, 7.6 us)
Async XLA Ops:
  6.5 46.1 %copy-start = (bf16[256,1024]{1,0:T(8,128)(2,1)S(1)}, bf16[256,1024]{1,0:T(8,128)(2,1)}, u32[]{:S(2)}) copy-start(bf16[256,1024]{1,0:T(8,128)(2,1)} %param.7) | copy-start | bytes 1572868
  6.5 65.4 %copy-start.1 = (bf16[256,1024]{1,0:T(8,128)(2,1)S(1)}, bf16[256,1024]{1,0:T(8,128)(2,1)}, u32[]{:S(2)}) copy-start(bf16[256,1024]{1,0:T(8,128)(2,1)} %param.8) | copy-start | bytes 1572868
  6.5 230.8 %all-gather.2.cloned.1.call-start = ((), (), s32[]{:S(2)}) async-start(), calls=%async_computation.8 | async-start | bytes 25559040 | tf_op jit(solution)/shard_map/all_gather | solution.py:68
  9.2 34.0 %all-to-all-start = ((bf16[1,256,8,128]{3,2,0,1:T(8,128)(2,1)}), bf16[1,256,8,128]{3,2,0,1:T(8,128)(2,1)S(1)}, u32[]{:S(2)}, u32[]{:S(2)}) async-start(bf16[1,256,8,128]{3,2,0,1:T(8,128)(2,1)} %bitcast.15), calls=%async_computation | async-start | bytes 1048576 | tf_op jit(solution)/shard_map/all_to_all | solution.py:48
  43.3 23.8 %all-to-all-start.1 = ((bf16[1,256,8,128]{3,2,0,1:T(8,128)(2,1)}), bf16[1,256,8,128]{3,2,0,1:T(8,128)(2,1)S(1)}, u32[]{:S(2)}, u32[]{:S(2)}) async-start(bf16[1,256,8,128]{3,2,0,1:T(8,128)(2,1)} %bitcast.19), calls=%async_computation.1 | async-start | bytes 1048576 | tf_op jit(solution)/shard_map/all_to_all | solution.py:49
  67.0 35.9 %all-to-all-start.3 = ((bf16[1,256,8,128]{3,2,0,1:T(8,128)(2,1)}), bf16[1,256,8,128]{3,2,0,1:T(8,128)(2,1)S(1)}, u32[]{:S(2)}, u32[]{:S(2)}) async-start(bf16[1,256,8,128]{3,2,0,1:T(8,128)(2,1)} %bitcast.27), calls=%async_computation.3 | async-start | bytes 1048576 | tf_op jit(solution)/shard_map/all_to_all | solution.py:50
  103.0 21.0 %all-to-all-start.2 = ((bf16[1,256,8,128]{3,2,0,1:T(8,128)(2,1)}), bf16[1,256,8,128]{3,2,0,1:T(8,128)(2,1)S(1)}, u32[]{:S(2)}, u32[]{:S(2)}) async-start(bf16[1,256,8,128]{3,2,0,1:T(8,128)(2,1)} %bitcast.23), calls=%async_computation.2 | async-start | bytes 1048576 | tf_op jit(solution)/shard_map/all_to_all | solution.py:51
  110.4 14.2 %copy-start.2 = (f32[4,8,64,64]{2,3,1,0:T(8,128)}, f32[4,8,64,64]{2,3,1,0:T(8,128)S(1)}, u32[]{:S(2)}) copy-start(f32[4,8,64,64]{2,3,1,0:T(8,128)S(1)} %get-tuple-element.6) | copy-start | bytes 1572868
  128.2 26.1 %all-to-all-start.5 = ((bf16[64,4,8,128]{3,2,1,0:T(8,128)(2,1)}), bf16[64,4,8,128]{3,2,1,0:T(8,128)(2,1)S(1)}, u32[]{:S(2)}, u32[]{:S(2)}) async-start(bf16[64,4,8,128]{3,2,1,0:T(8,128)(2,1)} %copy.38), calls=%async_computation.5 | async-start | bytes 1048576 | tf_op jit(solution)/shard_map/all_to_all | solution.py:56
  154.3 31.5 %all-to-all-start.4 = ((bf16[64,4,8,128]{3,2,1,0:T(8,128)(2,1)}), bf16[64,4,8,128]{3,2,1,0:T(8,128)(2,1)S(1)}, u32[]{:S(2)}, u32[]{:S(2)}) async-start(bf16[64,4,8,128]{3,2,1,0:T(8,128)(2,1)} %copy.36), calls=%async_computation.4 | async-start | bytes 1048576 | tf_op jit(solution)/shard_map/all_to_all | solution.py:55
  185.7 26.7 %all-to-all-start.6 = ((bf16[64,4,8,128]{3,2,1,0:T(8,128)(2,1)}), bf16[64,4,8,128]{3,2,1,0:T(8,128)(2,1)S(1)}, u32[]{:S(2)}, u32[]{:S(2)}) async-start(bf16[64,4,8,128]{3,2,1,0:T(8,128)(2,1)} %copy.40), calls=%async_computation.6 | async-start | bytes 1048576 | tf_op jit(solution)/shard_map/all_to_all | solution.py:57
  192.3 171.5 %reduce-scatter.2.cloned.1.call-start = ((), (), s32[]{:S(2)}) async-start(), calls=%async_computation.9 | async-start | bytes 5242880 | tf_op jit(solution)/shard_map/reduce_scatter | solution.py:72
Sparse Core Ops, SparseCore 0:
  10.7 226.5 all-gather.1
  251.2 112.5 reduce-scatter.1
where the time goes:
time: 374 us; the launch traced here: 373 us
  waiting for transfers between devices  268 us (72%)
  starting transfers between devices  60.2 us (16%)
  matrix products  19.4 us (5%)
  between operations  13.6 us (4%)
  local copies, waits for them, and re-layouts  10.8 us (3%)
    reduce_scatter x1, waiting for transfers between devices, per_device(): lax.psum_scatter(partial_sum, 'head', scatter_dimension=0, tiled=True)  113 us
    all_to_all x1, waiting for transfers between devices, per_device(): lax.all_to_all(sv, 'tm', split_axis=1, concat_axis=0, tiled=True)  30.1 us
    all_gather x1, waiting for transfers between devices, per_device(): lax.all_gather(weights, 'tm', axis=1, tiled=True)  24.6 us
    all_to_all x1, waiting for transfers between devices, per_device(): lax.all_to_all(grads[2], 'tm', split_axis=0, concat_axis=1, tiled=True)  19.5 us
    all_to_all x1, waiting for transfers between devices, per_device(): lax.all_to_all(grads[1], 'tm', split_axis=0, concat_axis=1, tiled=True)  18.6 us
    all_to_all x1, waiting for transfers between devices, per_device(): lax.all_to_all(grads[0], 'tm', split_axis=0, concat_axis=1, tiled=True)  17.4 us
    all_to_all x1, waiting for transfers between devices, per_device(): lax.all_to_all(sq, 'tm', split_axis=1, concat_axis=0, tiled=True)  17 us
    all_to_all x1, starting transfers between devices, per_device(): lax.all_to_all(sq, 'tm', split_axis=1, concat_axis=0, tiled=True)  15.1 us
  transfers between devices with their start and end apart: 9, of which 9 were waited for; matrix products, arithmetic and copies ran while one was open for 4% of the time, Pallas kernels for 0%

commit v1 on v0

--- a/solution.py
+++ b/solution.py
@@ -63,11 +63,14 @@
             back[2].reshape(tok_rows, width),
         ]
     )
+    detail_the_plane = lambda vals: jnp.concatenate(
+        jax.lax.all_to_all(
+            jnp.stack([vals for _ in range(jax.lax.axis_size("tm"))], 0), "tm", 0, 0
+        ),
+        1,
+    )
     partial_sum = jnp.einsum(
-        "mic,mtc->it",
-        lax.all_gather(weights, "tm", axis=1, tiled=True),
-        stacked,
-        preferred_element_type=jnp.float32,
+        "mic,mtc->it", detail_the_plane(weights), stacked, preferred_element_type=jnp.float32
     )
     mine = lax.psum_scatter(partial_sum, "head", scatter_dimension=0, tiled=True)
     return mine.astype(jnp.bfloat16)

time: 374 us -> 828 us (2.21)
  waiting for transfers between devices: 268 us -> 681 us
  local copies, waits for them, and re-layouts: 10.8 us -> 39.7 us
  blocking collectives: 0 us -> 17.9 us
    all_to_all x1, waiting for transfers between devices: 17.4 us -> 531 us  [per_device(): jax.lax.all_to_all(jnp.stack([vals for _ in range(jax.lax.axis_size('tm')...]
    reduce_scatter x1, waiting for transfers between devices: 113 us -> 69.2 us  [per_device(): lax.psum_scatter(partial_sum, 'head', scatter_dimension=0, tiled=True)]
    all_gather x1 -> x0, waiting for transfers between devices: 24.6 us -> none  [per_device(): lax.all_gather(weights, 'tm', axis=1, tiled=True)]
    reshape x0 -> x1, local copies, waits for them, and re-layouts: none -> 20.9 us  [per_device(): jnp.concatenate(jax.lax.all_to_all(jnp.stack([vals for _ in range(jax.lax...]
    all_to_all x1, waiting for transfers between devices: 30.1 us -> 10.4 us  [per_device(): lax.all_to_all(sv, 'tm', split_axis=1, concat_axis=0, tiled=True)]
    all_to_all x0 -> x1, blocking collectives: none -> 17.9 us  [per_device(): lax.all_to_all(grads[0], 'tm', split_axis=0, concat_axis=1, tiled=True)]
    all_to_all x1, waiting for transfers between devices: 19.5 us -> 9.82 us  [per_device(): lax.all_to_all(grads[2], 'tm', split_axis=0, concat_axis=1, tiled=True)]
    another operation x0 -> x1, local copies, waits for them, and re-layouts: none -> 8.73 us  [per_device(): jnp.stack([vals for _ in range(jax.lax.axis_size('tm'))], 0)]
  transfers between devices with their start and end apart: 9 -> 8, of which waited for: 9 -> 8; matrix products, arithmetic and copies ran while one was open for 4% -> 2% of each run, Pallas kernels for 0% -> 0%
where the time goes in v1:
time: 828 us; the launch traced here: 827 us
  waiting for transfers between devices  681 us (82%)
  starting transfers between devices  53.8 us (6%)
  local copies, waits for them, and re-layouts  39.7 us (5%)
  matrix products  20.1 us (2%)
  blocking collectives  17.9 us (2%)
  between operations  13.6 us (2%)
    all_to_all x1, waiting for transfers between devices, per_device(): jax.lax.all_to_all(jnp.stack([vals for _ in range(jax.lax.axis_size('tm')...  531 us
    reduce_scatter x1, waiting for transfers between devices, per_device(): lax.psum_scatter(partial_sum, 'head', scatter_dimension=0, tiled=True)  69.2 us
    reshape x1, local copies, waits for them, and re-layouts, per_device(): jnp.concatenate(jax.lax.all_to_all(jnp.stack([vals for _ in range(jax.lax...  20.9 us
    all_to_all x1, blocking collectives, per_device(): lax.all_to_all(grads[0], 'tm', split_axis=0, concat_axis=1, tiled=True)  17.9 us
    all_to_all x1, waiting for transfers between devices, per_device(): lax.all_to_all(sk, 'tm', split_axis=1, concat_axis=0, tiled=True)  17.4 us
  transfers between devices with their start and end apart: 8, of which 8 were waited for; matrix products, arithmetic and copies ran while one was open for 2% of the time, Pallas kernels for 0%

profile of v1, /device:TPU:1, one launch (start us, length us, event | category | flops | bytes accessed | tf_op | source)
XLA Modules:
  0.0 827.1 jit_solution(4864762090781597983)
XLA Ops:
  6.5 2.0 copy.48
  8.6 15.1 %all-to-all-start.2 = ((bf16[1,256,8,128]{3,2,0,1:T(8,128)(2,1)}), bf16[1,256,8,128]{3,2,0,1:T(8,128)(2,1)S(1)}, u32[]{:S(2)}, u32[]{:S(2)}) async-start(bf16[1,256,8,128]{3,2,0,1:T(8,128)(2,1)} %bitcast.25), calls=%async_computation.2 | async-start | bytes 1048576 | tf_op jit(solution)/shard_map/all_to_all | solution.py:51
  23.7 1.9 copy.47
  25.6 14.9 %all-to-all-done.2 = bf16[1,256,8,128]{3,2,0,1:T(8,128)(2,1)S(1)} async-done(((bf16[1,256,8,128]{3,2,0,1:T(8,128)(2,1)}), bf16[1,256,8,128]{3,2,0,1:T(8,128)(2,1)S(1)}, u32[]{:S(2)}, u32[]{:S(2)}) %all-to-all-start.2) | async-done | bytes 524320 | tf_op jit(solution)/shard_map/all_to_all | solution.py:51
  40.6 8.0 all-to-all-start.1
  49.4 17.4 %all-to-all-done.1 = bf16[1,256,8,128]{3,2,0,1:T(8,128)(2,1)S(1)} async-done(((bf16[1,256,8,128]{3,2,0,1:T(8,128)(2,1)}), bf16[1,256,8,128]{3,2,0,1:T(8,128)(2,1)S(1)}, u32[]{:S(2)}, u32[]{:S(2)}) %all-to-all-start.1) | async-done | bytes 524320 | tf_op jit(solution)/shard_map/all_to_all | solution.py:49
  66.8 6.5 all-to-all-start
  74.3 14.8 %all-to-all-done = bf16[1,256,8,128]{3,2,0,1:T(8,128)(2,1)S(1)} async-done(((bf16[1,256,8,128]{3,2,0,1:T(8,128)(2,1)}), bf16[1,256,8,128]{3,2,0,1:T(8,128)(2,1)S(1)}, u32[]{:S(2)}, u32[]{:S(2)}) %all-to-all-start) | async-done | bytes 524320 | tf_op jit(solution)/shard_map/all_to_all | solution.py:48
  89.1 6.9 all-to-all-start.3
  96.0 1.6 fusion.39
  97.6 1.6 fusion.16
  100.3 10.4 %all-to-all-done.3 = bf16[1,256,8,128]{3,2,0,1:T(8,128)(2,1)S(1)} async-done(((bf16[1,256,8,128]{3,2,0,1:T(8,128)(2,1)}), bf16[1,256,8,128]{3,2,0,1:T(8,128)(2,1)S(1)}, u32[]{:S(2)}, u32[]{:S(2)}) %all-to-all-start.3) | async-done | bytes 524320 | tf_op jit(solution)/shard_map/all_to_all | solution.py:50
  110.7 6.5 all-to-all-start.6
  117.3 1.9 fusion.13
  121.3 9.8 %all-to-all-done.6 = bf16[64,4,8,128]{3,2,1,0:T(8,128)(2,1)S(1)} async-done(((bf16[64,4,8,128]{3,2,1,0:T(8,128)(2,1)}), bf16[64,4,8,128]{3,2,1,0:T(8,128)(2,1)S(1)}, u32[]{:S(2)}, u32[]{:S(2)}) %all-to-all-start.6) | async-done | bytes 524320 | tf_op jit(solution)/shard_map/all_to_all | solution.py:57
  131.1 4.6 all-to-all-start.5
  136.5 13.1 %all-to-all-done.5 = bf16[64,4,8,128]{3,2,1,0:T(8,128)(2,1)S(1)} async-done(((bf16[64,4,8,128]{3,2,1,0:T(8,128)(2,1)}), bf16[64,4,8,128]{3,2,1,0:T(8,128)(2,1)S(1)}, u32[]{:S(2)}, u32[]{:S(2)}) %all-to-all-start.5) | async-done | bytes 524320 | tf_op jit(solution)/shard_map/all_to_all | solution.py:56
  149.6 17.9 %all_to_all.80 = bf16[64,4,8,128]{3,2,1,0:T(8,128)(2,1)S(1)} all-to-all(bf16[64,4,8,128]{3,2,1,0:T(8,128)(2,1)S(1)} %copy.36), channel_id=1, replica_groups=mesh['tm'=64,'head'=4] {'tm'}, dimensions={0} | all-to-all | bytes 1048576 | tf_op jit(solution)/shard_map/all_to_all | solution.py:55
  167.4 8.7 %stack.5 = bf16[64,3,64,1024]{3,2,1,0:T(8,128)(2,1)} broadcast(bf16[3,64,1024]{2,1,0:T(8,128)(2,1)S(1)} %copy-done.2), dimensions={1,2,3} | broadcast | bytes 25559040 | tf_op jit(solution)/shard_map/stack | solution.py:68
  176.2 6.1 all-to-all-start.7
  183.0 531.1 %all-to-all-done.7 = bf16[64,3,64,1024]{3,2,1,0:T(8,128)(2,1)} async-done(((bf16[64,3,64,1024]{3,2,1,0:T(8,128)(2,1)}), bf16[64,3,64,1024]{3,2,1,0:T(8,128)(2,1)}, u32[]{:S(2)}, u32[]{:S(2)}) %all-to-all-start.7) | async-done | bytes 25165856 | tf_op jit(solution)/shard_map/all_to_all | solution.py:67
  714.1 20.9 %copy.41 = bf16[3,64,64,1024]{3,2,1,0:T(8,128)(2,1)} copy(bf16[3,64,64,1024]{3,2,0,1:T(8,128)(2,1)} %bitcast.9) | data formatting | bytes 50331648 | tf_op jit(solution)/shard_map/reshape | solution.py:66
  735.0 13.8 %convolution_bitcast_fusion = f32[4096,256]{0,1:T(8,128)} fusion(bf16[3,4096,1024]{2,1,0:T(8,128)(2,1)} %bitcast.48, bf16[1,256,1024]{2,1,0:T(8,128)(2,1)S(1)} %stack_reshape.11, bf16[1,256,1024]{2,1,0:T(8,128)(2,1)S(1)} %stack_reshape.10, bf16[1,256,1024]{2,1,0:T(8,128)(2,1)S(1)} %stack_reshape.9), kind=kOutput, calls=%fused_computation.1 | convolution fusion | flops 6444023808 | bytes 30932992 | tf_op jit(solution)/shard_map/mic,mtc->it/dot_general | solution.py:72
  748.8 69.2 %reduce-scatter.2.cloned.1.call-done = f32[1024,256]{0,1:T(8,128)} async-done(((f32[4096,256]{0,1:T(8,128)}), f32[1024,256]{0,1:T(8,128)}) %reduce-scatter.2.cloned.1.call-update) | async-done | bytes 1048592 | tf_op jit(solution)/shard_map/reduce_scatter | solution.py:75
  (23 shorter events, 8.8 us)
Async XLA Ops:
  6.5 42.0 %copy-start = (bf16[256,1024]{1,0:T(8,128)(2,1)S(1)}, bf16[256,1024]{1,0:T(8,128)(2,1)}, u32[]{:S(2)}) copy-start(bf16[256,1024]{1,0:T(8,128)(2,1)} %param.5) | copy-start | bytes 1572868
  6.5 66.8 %copy-start.1 = (bf16[256,1024]{1,0:T(8,128)(2,1)S(1)}, bf16[256,1024]{1,0:T(8,128)(2,1)}, u32[]{:S(2)}) copy-start(bf16[256,1024]{1,0:T(8,128)(2,1)} %param.7) | copy-start | bytes 1572868
  8.6 32.0 %all-to-all-start.2 = ((bf16[1,256,8,128]{3,2,0,1:T(8,128)(2,1)}), bf16[1,256,8,128]{3,2,0,1:T(8,128)(2,1)S(1)}, u32[]{:S(2)}, u32[]{:S(2)}) async-start(bf16[1,256,8,128]{3,2,0,1:T(8,128)(2,1)} %bitcast.25), calls=%async_computation.2 | async-start | bytes 1048576 | tf_op jit(solution)/shard_map/all_to_all | solution.py:51
  40.6 26.3 %all-to-all-start.1 = ((bf16[1,256,8,128]{3,2,0,1:T(8,128)(2,1)}), bf16[1,256,8,128]{3,2,0,1:T(8,128)(2,1)S(1)}, u32[]{:S(2)}, u32[]{:S(2)}) async-start(bf16[1,256,8,128]{3,2,0,1:T(8,128)(2,1)} %bitcast.21), calls=%async_computation.1 | async-start | bytes 1048576 | tf_op jit(solution)/shard_map/all_to_all | solution.py:49
  66.8 22.3 %all-to-all-start = ((bf16[1,256,8,128]{3,2,0,1:T(8,128)(2,1)}), bf16[1,256,8,128]{3,2,0,1:T(8,128)(2,1)S(1)}, u32[]{:S(2)}, u32[]{:S(2)}) async-start(bf16[1,256,8,128]{3,2,0,1:T(8,128)(2,1)} %bitcast.17), calls=%async_computation | async-start | bytes 1048576 | tf_op jit(solution)/shard_map/all_to_all | solution.py:48
  89.1 21.6 %all-to-all-start.3 = ((bf16[1,256,8,128]{3,2,0,1:T(8,128)(2,1)}), bf16[1,256,8,128]{3,2,0,1:T(8,128)(2,1)S(1)}, u32[]{:S(2)}, u32[]{:S(2)}) async-start(bf16[1,256,8,128]{3,2,0,1:T(8,128)(2,1)} %bitcast.29), calls=%async_computation.3 | async-start | bytes 1048576 | tf_op jit(solution)/shard_map/all_to_all | solution.py:50
  110.7 20.4 %all-to-all-start.6 = ((bf16[64,4,8,128]{3,2,1,0:T(8,128)(2,1)}), bf16[64,4,8,128]{3,2,1,0:T(8,128)(2,1)S(1)}, u32[]{:S(2)}, u32[]{:S(2)}) async-start(bf16[64,4,8,128]{3,2,1,0:T(8,128)(2,1)} %copy.40), calls=%async_computation.6 | async-start | bytes 1048576 | tf_op jit(solution)/shard_map/all_to_all | solution.py:57
  117.3 2.0 copy-start.3
  119.8 47.6 %copy-start.2 = (bf16[3,64,1024]{2,1,0:T(8,128)(2,1)S(1)}, bf16[3,64,1024]{2,1,0:T(8,128)(2,1)}, u32[]{:S(2)}) copy-start(bf16[3,64,1024]{2,1,0:T(8,128)(2,1)} %param.9) | copy-start | bytes 1179652
  131.1 18.5 %all-to-all-start.5 = ((bf16[64,4,8,128]{3,2,1,0:T(8,128)(2,1)}), bf16[64,4,8,128]{3,2,1,0:T(8,128)(2,1)S(1)}, u32[]{:S(2)}, u32[]{:S(2)}) async-start(bf16[64,4,8,128]{3,2,1,0:T(8,128)(2,1)} %copy.38), calls=%async_computation.5 | async-start | bytes 1048576 | tf_op jit(solution)/shard_map/all_to_all | solution.py:56
  176.2 538.0 %all-to-all-start.7 = ((bf16[64,3,64,1024]{3,2,1,0:T(8,128)(2,1)}), bf16[64,3,64,1024]{3,2,1,0:T(8,128)(2,1)}, u32[]{:S(2)}, u32[]{:S(2)}) async-start(bf16[64,3,64,1024]{3,2,1,0:T(8,128)(2,1)} %stack.5), calls=%async_computation.7 | async-start | bytes 50331648 | tf_op jit(solution)/shard_map/all_to_all | solution.py:67
  182.3 635.7 %reduce-scatter.2.cloned.1.call-start = ((), (), s32[]{:S(2)}) async-start(), calls=%async_computation.9 | async-start | bytes 5242880 | tf_op jit(solution)/shard_map/reduce_scatter | solution.py:75
Sparse Core Ops, SparseCore 0:
  749.0 68.9 reduce-scatter.1
